TPU v7x, 128 devices: a whole 4x4x4 slice. The times are simulated.
128 devices in a mesh: tm: 32 (over z, y, core), row: 4 (over x).
Axes of the slice: x: 4, y: 4, z: 4, core: 2. Of those that a mesh axis runs over, the one named last changes fastest.
Arguments:
- edge_factor: float32 [32, 512, 512], P('tm', 'row'), may hold values from -0.25 to 0.25
- mass: float32 [32, 512], P('tm', 'row'), may hold values from 0.001 to 0.01
- rhs: float32 [32, 512, 512], P('tm', None, 'row'), may hold values from -0.25 to 0.25
Outputs:
- solution: float32 [32, 512, 512], P('tm', None, 'row')
All inputs are finite; a program needn't handle non-finite values.
Results may differ from a plain program's by a relative error of at most 0.0003.
Values sent between devices are 32-bit elements; how exact they have to be, the bound alone decides.
A program may use at most 128 MiB of HBM per device.

v0:
```python
import jax
import jax.numpy as jnp
from jax import lax
from jax.sharding import PartitionSpec as P

exact_prec = lax.Precision.HIGHEST


def passed_along(block, axis, distance):
    devices = range(lax.axis_size(axis))
    route = [(i - distance, i) for i in devices if i - distance in devices]
    return lax.ppermute(block, axis, route)


def solve_lower(factor, values):
    return jax.scipy.linalg.solve_triangular(factor, values, lower=True)


def block_cholesky(matrix):
    half = matrix.shape[0] // 2
    upper_left = jnp.linalg.cholesky(matrix[:half, :half])
    lower_left = solve_lower(upper_left, matrix[:half, half:]).T
    schur_part = matrix[half:, half:] - jnp.dot(lower_left, lower_left.T, precision=exact_prec)
    lower_right = jnp.linalg.cholesky(schur_part)
    top_rows = jnp.concatenate(
        [upper_left, jnp.zeros((half, matrix.shape[0] - half), jnp.float32)], axis=1
    )
    bottom_rows = jnp.concatenate([lower_left, lower_right], axis=1)
    return jnp.concatenate([top_rows, bottom_rows], axis=0)


def factor_split(diag_part):
    full_diag = lax.all_gather(diag_part, "row", axis=1, tiled=True)
    return block_cholesky(full_diag)


def local(edge_factor, mass, rhs):
    factor_rows = edge_factor[0]
    mass_rows = mass[0]
    rhs_cols = rhs[0]
    quarter = factor_rows.shape[0]
    node_count = factor_rows.shape[1]
    blocks = lax.axis_size("tm")
    at_start = lax.axis_index("tm") == 0
    edge_cols = jnp.dot(
        lax.all_gather(factor_rows, "row", axis=0, tiled=True),
        factor_rows.T,
        precision=exact_prec,
        preferred_element_type=jnp.float32,
    )
    edge_next = passed_along(edge_cols, "tm", -1)
    offset = lax.axis_index("row") * quarter
    row_ids = lax.broadcasted_iota(jnp.int32, (node_count, quarter), 0)
    col_ids = lax.broadcasted_iota(jnp.int32, (node_count, quarter), 1) + offset
    mass_diag = jnp.where(row_ids == col_ids, mass_rows[None, :], 0.0)
    diag_part = mass_diag + edge_cols + edge_next
    low_coupling = jnp.where(at_start, 0.0, -edge_cols)
    up_coupling = -edge_next
    stride = 1
    while stride < blocks:
        factor = factor_split(diag_part)
        whitened = solve_lower(
            factor, jnp.concatenate([low_coupling, up_coupling, rhs_cols], axis=1)
        )
        stacked = jnp.stack([whitened[:, :quarter], whitened[:, quarter : 2 * quarter]])
        gram_blocks = jnp.einsum(
            "tbn,bk->tnk",
            lax.all_gather(stacked, "row", axis=2, tiled=True),
            whitened,
            precision=exact_prec,
        )
        from_below = passed_along(gram_blocks[1], "tm", stride)
        from_above = passed_along(gram_blocks[0], "tm", -stride)
        diag_part = diag_part - from_below[:, quarter : 2 * quarter] - from_above[:, :quarter]
        low_coupling = -from_below[:, :quarter]
        up_coupling = -from_above[:, quarter : 2 * quarter]
        rhs_cols = rhs_cols - from_below[:, 2 * quarter :] - from_above[:, 2 * quarter :]
        stride = stride * 2
    factor = factor_split(diag_part)
    inner = solve_lower(factor, rhs_cols)
    solution = jax.scipy.linalg.solve_triangular(factor, inner, lower=True, trans=1)
    return solution[None]


def solution(mesh):
    placed = (P("tm", "row", None), P("tm", "row"), P("tm", None, "row"))
    return jax.shard_map(
        local, mesh=mesh, in_specs=placed, out_specs=P("tm", None, "row"), check_vma=False
    )
```

profile of v0, /device:TPU:0, one launch (start us, length us, event | category | flops | bytes accessed | tf_op | source)
XLA Modules:
  0.0 1456.5 jit_solution(16818976105928106084)
XLA Ops:
  7.3 28.3 %all-gather.36.cloned.1.call-done = f32[1,512,512]{2,1,0:T(8,128)} async-done(((f32[1,128,512]{2,1,0:T(8,128)}), f32[1,512,512]{2,1,0:T(8,128)}) %all-gather.36.cloned.1.call-update) | async-done | bytes 1048592 | tf_op jit(solution)/shard_map/all_gather | solution.py:46
  43.3 28.3 %all-gather.14.cloned.1.call-done = f32[512,512]{0,1:T(8,128)} async-done(((f32[512,128]{0,1:T(8,128)}), f32[512,512]{0,1:T(8,128)}) %all-gather.14.cloned.1.call-update) | async-done | bytes 1048592 | tf_op jit(solution)/shard_map/all_gather | solution.py:33
  95.9 11.7 cholesky.567
  114.0 19.7 %custom-call.43 = f32[2,128,128]{1,2,0:T(8,128)S(1)} custom-call(f32[2,128,128]{2,1,0:T(8,128)S(1)} %get-tuple-element.86), custom_call_target="InvertDiagBlocksLowerTriangular" | custom-call | tf_op jit(solution)/shard_map/jit(_solve_triangular)/triangular_solve | solution.py:16
  180.4 39.8 %custom-call.45 = f32[4,128,128]{1,2,0:T(8,128)S(1)} custom-call(f32[4,128,128]{2,1,0:T(8,128)S(1)} %get-tuple-element.87), custom_call_target="InvertDiagBlocksLowerTriangular" | custom-call | tf_op jit(solution)/shard_map/jit(_solve_triangular)/triangular_solve | solution.py:16
  225.3 34.4 %all-gather.16.cloned.1.call-done = f32[2,512,512]{2,1,0:T(8,128)} async-done(((f32[2,512,128]{2,1,0:T(8,128)}), f32[2,512,512]{2,1,0:T(8,128)}) %all-gather.16.cloned.1.call-update) | async-done | bytes 2097168 | tf_op jit(solution)/shard_map/all_gather | solution.py:68
  272.6 35.7 %all-gather.18.cloned.1.call-done = f32[512,512]{0,1:T(8,128)} async-done(((f32[512,128]{0,1:T(8,128)}), f32[512,512]{0,1:T(8,128)}) %all-gather.18.cloned.1.call-update) | async-done | bytes 1048592 | tf_op jit(solution)/shard_map/all_gather | solution.py:33
  351.0 19.9 %custom-call.47 = f32[2,128,128]{1,2,0:T(8,128)S(1)} custom-call(f32[2,128,128]{2,1,0:T(8,128)S(1)} %get-tuple-element.88), custom_call_target="InvertDiagBlocksLowerTriangular" | custom-call | tf_op jit(solution)/shard_map/jit(_solve_triangular)/triangular_solve | solution.py:16
  417.6 39.7 %custom-call.49 = f32[4,128,128]{1,2,0:T(8,128)S(1)} custom-call(f32[4,128,128]{2,1,0:T(8,128)S(1)} %get-tuple-element.89), custom_call_target="InvertDiagBlocksLowerTriangular" | custom-call | tf_op jit(solution)/shard_map/jit(_solve_triangular)/triangular_solve | solution.py:16
  462.5 34.4 %all-gather.20.cloned.1.call-done = f32[2,512,512]{2,1,0:T(8,128)} async-done(((f32[2,512,128]{2,1,0:T(8,128)}), f32[2,512,512]{2,1,0:T(8,128)}) %all-gather.20.cloned.1.call-update) | async-done | bytes 2097168 | tf_op jit(solution)/shard_map/all_gather | solution.py:68
  506.1 14.1 collective-permute-done.3
  525.6 26.4 %all-gather.22.cloned.1.call-done = f32[512,512]{0,1:T(8,128)} async-done(((f32[512,128]{0,1:T(8,128)}), f32[512,512]{0,1:T(8,128)}) %all-gather.22.cloned.1.call-update) | async-done | bytes 1048592 | tf_op jit(solution)/shard_map/all_gather | solution.py:33
  594.7 19.9 %custom-call.51 = f32[2,128,128]{1,2,0:T(8,128)S(1)} custom-call(f32[2,128,128]{2,1,0:T(8,128)S(1)} %get-tuple-element.90), custom_call_target="InvertDiagBlocksLowerTriangular" | custom-call | tf_op jit(solution)/shard_map/jit(_solve_triangular)/triangular_solve | solution.py:16
  661.3 39.7 %custom-call.53 = f32[4,128,128]{1,2,0:T(8,128)S(1)} custom-call(f32[4,128,128]{2,1,0:T(8,128)S(1)} %get-tuple-element.91), custom_call_target="InvertDiagBlocksLowerTriangular" | custom-call | tf_op jit(solution)/shard_map/jit(_solve_triangular)/triangular_solve | solution.py:16
  706.1 34.4 %all-gather.24.cloned.1.call-done = f32[2,512,512]{2,1,0:T(8,128)} async-done(((f32[2,512,128]{2,1,0:T(8,128)}), f32[2,512,512]{2,1,0:T(8,128)}) %all-gather.24.cloned.1.call-update) | async-done | bytes 2097168 | tf_op jit(solution)/shard_map/all_gather | solution.py:68
  751.3 14.1 collective-permute-done.5
  765.3 18.8 %collective-permute-done.6 = f32[512,384]{0,1:T(8,128)S(1)} collective-permute-done((f32[512,384]{0,1:T(8,128)S(1)}, f32[512,384]{0,1:T(8,128)S(1)}, u32[]{:S(2)}, u32[]{:S(2)}) %collective-permute-start.6) | collective-permute-done | bytes 786464 | tf_op jit(solution)/shard_map/ppermute | solution.py:12
  785.4 24.6 %all-gather.26.cloned.1.call-done = f32[512,512]{0,1:T(8,128)} async-done(((f32[512,128]{0,1:T(8,128)}), f32[512,512]{0,1:T(8,128)}) %all-gather.26.cloned.1.call-update) | async-done | bytes 1048592 | tf_op jit(solution)/shard_map/all_gather | solution.py:33
  834.3 11.7 cholesky.771
  852.7 19.9 %custom-call.55 = f32[2,128,128]{1,2,0:T(8,128)S(1)} custom-call(f32[2,128,128]{2,1,0:T(8,128)S(1)} %get-tuple-element.92), custom_call_target="InvertDiagBlocksLowerTriangular" | custom-call | tf_op jit(solution)/shard_map/jit(_solve_triangular)/triangular_solve | solution.py:16
  919.4 39.7 %custom-call.57 = f32[4,128,128]{1,2,0:T(8,128)S(1)} custom-call(f32[4,128,128]{2,1,0:T(8,128)S(1)} %get-tuple-element.93), custom_call_target="InvertDiagBlocksLowerTriangular" | custom-call | tf_op jit(solution)/shard_map/jit(_solve_triangular)/triangular_solve | solution.py:16
  964.2 34.4 %all-gather.28.cloned.1.call-done = f32[2,512,512]{2,1,0:T(8,128)} async-done(((f32[2,512,128]{2,1,0:T(8,128)}), f32[2,512,512]{2,1,0:T(8,128)}) %all-gather.28.cloned.1.call-update) | async-done | bytes 2097168 | tf_op jit(solution)/shard_map/all_gather | solution.py:68
  1007.8 14.1 collective-permute-done.7
  1027.3 24.6 %all-gather.30.cloned.1.call-done = f32[512,512]{0,1:T(8,128)} async-done(((f32[512,128]{0,1:T(8,128)}), f32[512,512]{0,1:T(8,128)}) %all-gather.30.cloned.1.call-update) | async-done | bytes 1048592 | tf_op jit(solution)/shard_map/all_gather | solution.py:33
  1094.6 19.9 %custom-call.59 = f32[2,128,128]{1,2,0:T(8,128)S(1)} custom-call(f32[2,128,128]{2,1,0:T(8,128)S(1)} %get-tuple-element.94), custom_call_target="InvertDiagBlocksLowerTriangular" | custom-call | tf_op jit(solution)/shard_map/jit(_solve_triangular)/triangular_solve | solution.py:16
  1161.2 39.7 %custom-call.61 = f32[4,128,128]{1,2,0:T(8,128)S(1)} custom-call(f32[4,128,128]{2,1,0:T(8,128)S(1)} %get-tuple-element.95), custom_call_target="InvertDiagBlocksLowerTriangular" | custom-call | tf_op jit(solution)/shard_map/jit(_solve_triangular)/triangular_solve | solution.py:16
  1206.1 34.4 %all-gather.32.cloned.1.call-done = f32[2,512,512]{2,1,0:T(8,128)} async-done(((f32[2,512,128]{2,1,0:T(8,128)}), f32[2,512,512]{2,1,0:T(8,128)}) %all-gather.32.cloned.1.call-update) | async-done | bytes 2097168 | tf_op jit(solution)/shard_map/all_gather | solution.py:68
  1252.5 13.7 collective-permute-done.10
  1268.3 26.7 %all-gather.34.cloned.1.call-done = f32[512,512]{0,1:T(8,128)} async-done(((f32[512,128]{0,1:T(8,128)}), f32[512,512]{0,1:T(8,128)}) %all-gather.34.cloned.1.call-update) | async-done | bytes 1048592 | tf_op jit(solution)/shard_map/all_gather | solution.py:33
  1319.3 11.7 cholesky.907
  1337.5 19.9 %custom-call.63 = f32[2,128,128]{1,2,0:T(8,128)S(1)} custom-call(f32[2,128,128]{2,1,0:T(8,128)S(1)} %get-tuple-element.96), custom_call_target="InvertDiagBlocksLowerTriangular" | custom-call | tf_op jit(solution)/shard_map/jit(_solve_triangular)/triangular_solve | solution.py:16
  1404.5 39.6 %custom-call.21 = f32[4,128,128]{1,2,0:T(8,128)S(1)} custom-call(f32[4,128,128]{2,1,0:T(8,128)S(1)} %get-tuple-element.31), custom_call_target="InvertDiagBlocksLowerTriangular" | custom-call | tf_op jit(solution)/shard_map/jit(_solve_triangular)/triangular_solve | solution.py:81
  (514 shorter events, 663.5 us)
Async XLA Ops:
  6.5 36.5 %copy-start.11 = (f32[1,512,128]{2,1,0:T(8,128)S(1)}, f32[1,512,128]{2,1,0:T(8,128)}, u32[]{:S(2)}) copy-start(f32[1,512,128]{2,1,0:T(8,128)} %param.10) | copy-start | bytes 786436
  6.5 29.1 %all-gather.36.cloned.1.call-start = ((), (), s32[]{:S(2)}) async-start(), calls=%async_computation.11 | async-start | bytes 1310720 | tf_op jit(solution)/shard_map/all_gather | solution.py:46
  7.3 64.4 %all-gather.14.cloned.1.call-start = ((), (), s32[]{:S(2)}) async-start(), calls=%async_computation | async-start | bytes 1310720 | tf_op jit(solution)/shard_map/all_gather | solution.py:33
  38.0 3.4 collective-permute-start
  43.0 216.7 %all-gather.16.cloned.1.call-start = ((), (), s32[]{:S(2)}) async-start(), calls=%async_computation.1 | async-start | bytes 2621440 | tf_op jit(solution)/shard_map/all_gather | solution.py:68
  72.6 61.1 %copy-start.5 = (f32[512,512]{0,1:T(8,128)S(1)}, f32[512,512]{0,1:T(8,128)}, u32[]{:S(2)}) copy-start(f32[512,512]{0,1:T(8,128)} %all-gather.14.cloned.1.call-done) | copy-start | bytes 3145732
  225.2 83.1 %all-gather.18.cloned.1.call-start = ((), (), s32[]{:S(2)}) async-start(), calls=%async_computation.2 | async-start | bytes 1310720 | tf_op jit(solution)/shard_map/all_gather | solution.py:33
  264.1 3.2 collective-permute-start.1
  265.5 5.9 collective-permute-start.2
  272.3 224.5 %all-gather.20.cloned.1.call-start = ((), (), s32[]{:S(2)}) async-start(), calls=%async_computation.3 | async-start | bytes 2621440 | tf_op jit(solution)/shard_map/all_gather | solution.py:68
  309.3 61.6 %copy-start.6 = (f32[512,512]{0,1:T(8,128)S(1)}, f32[512,512]{0,1:T(8,128)}, u32[]{:S(2)}) copy-start(f32[512,512]{0,1:T(8,128)} %all-gather.18.cloned.1.call-done) | copy-start | bytes 3145732
  462.4 89.5 %all-gather.22.cloned.1.call-start = ((), (), s32[]{:S(2)}) async-start(), calls=%async_computation.4 | async-start | bytes 1310720 | tf_op jit(solution)/shard_map/all_gather | solution.py:33
  501.3 18.8 %collective-permute-start.3 = (f32[512,384]{0,1:T(8,128)S(1)}, f32[512,384]{0,1:T(8,128)S(1)}, u32[]{:S(2)}, u32[]{:S(2)}) collective-permute-start(f32[512,384]{0,1:T(8,128)S(1)} %get-tuple-element.243), channel_id=1, source_target_pairs={{0,8},{4,12},{8,16},{12,20},{16,24},{20,28},{24,32},{28,36},{32,40... | collective-permute-start | bytes 2359304 | tf_op jit(solution)/shard_map/ppermute | solution.py:12
  504.8 19.5 %collective-permute-start.4 = (f32[512,384]{0,1:T(8,128)S(1)}, f32[512,384]{0,1:T(8,128)S(1)}, u32[]{:S(2)}, u32[]{:S(2)}) collective-permute-start(f32[512,384]{0,1:T(8,128)S(1)} %get-tuple-element.244), channel_id=1, source_target_pairs={{8,0},{12,4},{16,8},{20,12},{24,16},{28,20},{32,24},{36,28},{40,32... | collective-permute-start | bytes 2359304 | tf_op jit(solution)/shard_map/ppermute | solution.py:12
  525.3 215.2 %all-gather.24.cloned.1.call-start = ((), (), s32[]{:S(2)}) async-start(), calls=%async_computation.5 | async-start | bytes 2621440 | tf_op jit(solution)/shard_map/all_gather | solution.py:68
  552.9 61.6 %copy-start.7 = (f32[512,512]{0,1:T(8,128)S(1)}, f32[512,512]{0,1:T(8,128)}, u32[]{:S(2)}) copy-start(f32[512,512]{0,1:T(8,128)} %all-gather.22.cloned.1.call-done) | copy-start | bytes 3145732
  706.1 103.9 %all-gather.26.cloned.1.call-start = ((), (), s32[]{:S(2)}) async-start(), calls=%async_computation.6 | async-start | bytes 1310720 | tf_op jit(solution)/shard_map/all_gather | solution.py:33
  744.8 39.3 %copy-start.1 = (f32[512,128]{0,1:T(8,128)S(1)}, f32[512,128]{0,1:T(8,128)}, u32[]{:S(2)}) copy-start(f32[512,128]{0,1:T(8,128)} %get-tuple-element.241) | copy-start | bytes 786436
  745.0 20.3 %collective-permute-start.5 = (f32[512,384]{0,1:T(8,128)S(1)}, f32[512,384]{0,1:T(8,128)S(1)}, u32[]{:S(2)}, u32[]{:S(2)}) collective-permute-start(f32[512,384]{0,1:T(8,128)S(1)} %get-tuple-element.239), channel_id=1, source_target_pairs={{0,16},{4,20},{8,24},{12,28},{16,32},{20,36},{24,40},{28,44},{32,4... | collective-permute-start | bytes 2359304 | tf_op jit(solution)/shard_map/ppermute | solution.py:12
  750.0 34.2 %collective-permute-start.6 = (f32[512,384]{0,1:T(8,128)S(1)}, f32[512,384]{0,1:T(8,128)S(1)}, u32[]{:S(2)}, u32[]{:S(2)}) collective-permute-start(f32[512,384]{0,1:T(8,128)S(1)} %get-tuple-element.240), channel_id=1, source_target_pairs={{16,0},{20,4},{24,8},{28,12},{32,16},{36,20},{40,24},{44,28},{48,3... | collective-permute-start | bytes 2359304 | tf_op jit(solution)/shard_map/ppermute | solution.py:12
  785.1 213.4 %all-gather.28.cloned.1.call-start = ((), (), s32[]{:S(2)}) async-start(), calls=%async_computation.7 | async-start | bytes 2621440 | tf_op jit(solution)/shard_map/all_gather | solution.py:68
  811.0 61.6 %copy-start.8 = (f32[512,512]{0,1:T(8,128)S(1)}, f32[512,512]{0,1:T(8,128)}, u32[]{:S(2)}) copy-start(f32[512,512]{0,1:T(8,128)} %all-gather.26.cloned.1.call-done) | copy-start | bytes 3145732
  964.1 87.8 %all-gather.30.cloned.1.call-start = ((), (), s32[]{:S(2)}) async-start(), calls=%async_computation.8 | async-start | bytes 1310720 | tf_op jit(solution)/shard_map/all_gather | solution.py:33
  1002.9 23.2 %copy-start.2 = (f32[512,128]{0,1:T(8,128)S(1)}, f32[512,128]{0,1:T(8,128)}, u32[]{:S(2)}) copy-start(f32[512,128]{0,1:T(8,128)} %get-tuple-element.237) | copy-start | bytes 786436
  1003.0 18.9 %collective-permute-start.7 = (f32[512,384]{0,1:T(8,128)S(1)}, f32[512,384]{0,1:T(8,128)S(1)}, u32[]{:S(2)}, u32[]{:S(2)}) collective-permute-start(f32[512,384]{0,1:T(8,128)S(1)} %get-tuple-element.235), channel_id=1, source_target_pairs={{0,32},{4,36},{8,40},{12,44},{16,48},{20,52},{24,56},{28,60},{32,6... | collective-permute-start | bytes 2359304 | tf_op jit(solution)/shard_map/ppermute | solution.py:12
  1006.5 19.5 %collective-permute-start.8 = (f32[512,384]{0,1:T(8,128)S(1)}, f32[512,384]{0,1:T(8,128)S(1)}, u32[]{:S(2)}, u32[]{:S(2)}) collective-permute-start(f32[512,384]{0,1:T(8,128)S(1)} %get-tuple-element.236), channel_id=1, source_target_pairs={{32,0},{36,4},{40,8},{44,12},{48,16},{52,20},{56,24},{60,28},{64,3... | collective-permute-start | bytes 2359304 | tf_op jit(solution)/shard_map/ppermute | solution.py:12
  1027.0 213.4 %all-gather.32.cloned.1.call-start = ((), (), s32[]{:S(2)}) async-start(), calls=%async_computation.9 | async-start | bytes 2621440 | tf_op jit(solution)/shard_map/all_gather | solution.py:68
  1052.9 61.6 %copy-start.9 = (f32[512,512]{0,1:T(8,128)S(1)}, f32[512,512]{0,1:T(8,128)}, u32[]{:S(2)}) copy-start(f32[512,512]{0,1:T(8,128)} %all-gather.30.cloned.1.call-done) | copy-start | bytes 3145732
  1206.0 89.0 %all-gather.34.cloned.1.call-start = ((), (), s32[]{:S(2)}) async-start(), calls=%async_computation.10 | async-start | bytes 1310720 | tf_op jit(solution)/shard_map/all_gather | solution.py:33
  1244.9 21.3 %collective-permute-start.10 = (f32[512,384]{0,1:T(8,128)S(1)}, f32[512,384]{0,1:T(8,128)S(1)}, u32[]{:S(2)}, u32[]{:S(2)}) collective-permute-start(f32[512,384]{0,1:T(8,128)S(1)} %get-tuple-element.232), channel_id=1, source_target_pairs={{64,0},{68,4},{72,8},{76,12},{80,16},{84,20},{88,24},{92,28},{96,3... | collective-permute-start | bytes 2359304 | tf_op jit(solution)/shard_map/ppermute | solution.py:12
  1246.2 21.2 %collective-permute-start.9 = (f32[512,384]{0,1:T(8,128)S(1)}, f32[512,384]{0,1:T(8,128)S(1)}, u32[]{:S(2)}, u32[]{:S(2)}) collective-permute-start(f32[512,384]{0,1:T(8,128)S(1)} %get-tuple-element.231), channel_id=1, source_target_pairs={{0,64},{4,68},{8,72},{12,76},{16,80},{20,84},{24,88},{28,92},{32,9... | collective-permute-start | bytes 2359304 | tf_op jit(solution)/shard_map/ppermute | solution.py:12
  1296.0 61.3 %copy-start.10 = (f32[512,512]{0,1:T(8,128)S(1)}, f32[512,512]{0,1:T(8,128)}, u32[]{:S(2)}) copy-start(f32[512,512]{0,1:T(8,128)} %all-gather.34.cloned.1.call-done) | copy-start | bytes 3145732
  (3 other events, 53.1 us)
Sparse Core Ops, SparseCore 0:
  9.0 26.5 all-gather.35
  43.1 28.4 all-gather.13
  225.3 34.2 all-gather.15
  272.4 35.8 all-gather.17
  462.5 34.2 all-gather.19
  525.4 26.5 all-gather.21
  706.2 34.2 all-gather.23
  785.2 24.7 all-gather.25
  964.2 34.2 all-gather.27
  1027.2 24.6 all-gather.29
  1206.1 34.2 all-gather.31
  1268.5 26.5 all-gather.33
where the time goes:
time: 1470 us; the launch traced here: 1460 us
  other arithmetic  792 us (54%)
  waiting for transfers between devices  458 us (31%)
  local copies, waits for them, and re-layouts  82.2 us (6%)
  matrix products  63.1 us (4%)
  between operations  31.4 us (2%)
  starting transfers between devices  28.5 us (2%)
    another operation x29, other arithmetic, solve_lower(): return jax.scipy.linalg.solve_triangular(factor, values, lower=True)  319 us
    another operation x42, other arithmetic, block_cholesky(): lower_right = jnp.linalg.cholesky(schur_part)  208 us
    another operation x41, other arithmetic, block_cholesky(): upper_left = jnp.linalg.cholesky(matrix[:half, :half])  207 us
    all_gather x5, waiting for transfers between devices, local(): lax.all_gather(stacked, 'row', axis=2, tiled=True)  172 us
    all_gather x6, waiting for transfers between devices, factor_split(): full_diag = lax.all_gather(diag_part, 'row', axis=1, tiled=True)  166 us
    ppermute x11, waiting for transfers between devices, passed_along(): return lax.ppermute(block, axis, route)  90.9 us
    another operation x116, local copies, waits for them, and re-layouts, solve_lower(): return jax.scipy.linalg.solve_triangular(factor, values, lower=True)  64.6 us
    another operation x2, other arithmetic, local(): jax.scipy.linalg.solve_triangular(factor, inner, lower=True, trans=1)  39.7 us
  transfers between devices with their start and end apart: 23, of which 23 were waited for; matrix products, arithmetic and copies ran while one was open for 0% of the time, Pallas kernels for 0%

commit v1 on v0

--- a/solution.py
+++ b/solution.py
@@ -30,7 +30,8 @@
 
 
 def factor_split(diag_part):
-    full_diag = lax.all_gather(diag_part, "row", axis=1, tiled=True)
+    stack = jnp.stack([diag_part] * lax.axis_size("row"))
+    full_diag = jnp.concatenate(lax.all_to_all(stack, "row", 0, 0), axis=1)
     return block_cholesky(full_diag)
 
 

time: 1470 us -> 1400 us (0.952)
  waiting for transfers between devices: 458 us -> 381 us
  starting transfers between devices: 28.5 us -> 51.3 us
    all_gather x6 -> x0, waiting for transfers between devices: 166 us -> none  [factor_split(): full_diag = lax.all_gather(diag_part, 'row', axis=1, tiled=True)]
    all_to_all x0 -> x6, waiting for transfers between devices: none -> 73.6 us  [factor_split(): full_diag = jnp.concatenate(lax.all_to_all(stack, 'row', 0, 0), axis=1)]
    all_to_all x0 -> x6, starting transfers between devices: none -> 23.4 us  [factor_split(): full_diag = jnp.concatenate(lax.all_to_all(stack, 'row', 0, 0), axis=1)]
    all_gather x5, waiting for transfers between devices: 172 us -> 187 us  [local(): lax.all_gather(stacked, 'row', axis=2, tiled=True)]
where the time goes in v1:
time: 1400 us; the launch traced here: 1390 us
  other arithmetic  782 us (56%)
  waiting for transfers between devices  381 us (27%)
  local copies, waits for them, and re-layouts  83.9 us (6%)
  matrix products  63.1 us (5%)
  starting transfers between devices  51.3 us (4%)
  between operations  31.5 us (2%)
    another operation x29, other arithmetic, solve_lower(): return jax.scipy.linalg.solve_triangular(factor, values, lower=True)  319 us
    another operation x42, other arithmetic, block_cholesky(): lower_right = jnp.linalg.cholesky(schur_part)  208 us
    another operation x41, other arithmetic, block_cholesky(): upper_left = jnp.linalg.cholesky(matrix[:half, :half])  207 us
    all_gather x5, waiting for transfers between devices, local(): lax.all_gather(stacked, 'row', axis=2, tiled=True)  187 us
    ppermute x11, waiting for transfers between devices, passed_along(): return lax.ppermute(block, axis, route)  91.1 us
    all_to_all x6, waiting for transfers between devices, factor_split(): full_diag = jnp.concatenate(lax.all_to_all(stack, 'row', 0, 0), axis=1)  73.6 us
    another operation x116, local copies, waits for them, and re-layouts, solve_lower(): return jax.scipy.linalg.solve_triangular(factor, values, lower=True)  65.2 us
    another operation x2, other arithmetic, local(): jax.scipy.linalg.solve_triangular(factor, inner, lower=True, trans=1)  39.7 us
  transfers between devices with their start and end apart: 23, of which 23 were waited for; matrix products, arithmetic and copies ran while one was open for 0% of the time, Pallas kernels for 0%

profile of v1, /device:TPU:0, one launch (start us, length us, event | category | flops | bytes accessed | tf_op | source)
XLA Modules:
  0.0 1393.0 jit_solution(1849286465798100265)
XLA Ops:
  7.3 28.3 %all-gather.18.cloned.1.call-done = f32[1,512,512]{2,1,0:T(8,128)} async-done(((f32[1,128,512]{2,1,0:T(8,128)}), f32[1,512,512]{2,1,0:T(8,128)}) %all-gather.18.cloned.1.call-update) | async-done | bytes 1048592 | tf_op jit(solution)/shard_map/all_gather | solution.py:47
  47.2 13.0 all-to-all-done
  82.6 11.7 cholesky.567
  100.7 19.7 %custom-call.43 = f32[2,128,128]{1,2,0:T(8,128)S(1)} custom-call(f32[2,128,128]{2,1,0:T(8,128)S(1)} %get-tuple-element.86), custom_call_target="InvertDiagBlocksLowerTriangular" | custom-call | tf_op jit(solution)/shard_map/jit(_solve_triangular)/triangular_solve | solution.py:16
  167.1 39.8 %custom-call.45 = f32[4,128,128]{1,2,0:T(8,128)S(1)} custom-call(f32[4,128,128]{2,1,0:T(8,128)S(1)} %get-tuple-element.87), custom_call_target="InvertDiagBlocksLowerTriangular" | custom-call | tf_op jit(solution)/shard_map/jit(_solve_triangular)/triangular_solve | solution.py:16
  212.0 38.5 %all-gather.8.cloned.1.call-done = f32[2,512,512]{2,1,0:T(8,128)} async-done(((f32[2,512,128]{2,1,0:T(8,128)}), f32[2,512,512]{2,1,0:T(8,128)}) %all-gather.8.cloned.1.call-update) | async-done | bytes 2097168 | tf_op jit(solution)/shard_map/all_gather | solution.py:69
  300.7 11.7 cholesky.635
  319.2 19.9 %custom-call.47 = f32[2,128,128]{1,2,0:T(8,128)S(1)} custom-call(f32[2,128,128]{2,1,0:T(8,128)S(1)} %get-tuple-element.88), custom_call_target="InvertDiagBlocksLowerTriangular" | custom-call | tf_op jit(solution)/shard_map/jit(_solve_triangular)/triangular_solve | solution.py:16
  385.8 39.7 %custom-call.49 = f32[4,128,128]{1,2,0:T(8,128)S(1)} custom-call(f32[4,128,128]{2,1,0:T(8,128)S(1)} %get-tuple-element.89), custom_call_target="InvertDiagBlocksLowerTriangular" | custom-call | tf_op jit(solution)/shard_map/jit(_solve_triangular)/triangular_solve | solution.py:16
  430.6 46.8 %all-gather.10.cloned.1.call-done = f32[2,512,512]{2,1,0:T(8,128)} async-done(((f32[2,512,128]{2,1,0:T(8,128)}), f32[2,512,512]{2,1,0:T(8,128)}) %all-gather.10.cloned.1.call-update) | async-done | bytes 2097168 | tf_op jit(solution)/shard_map/all_gather | solution.py:69
  486.6 14.1 %collective-permute-done.3 = f32[512,384]{0,1:T(8,128)S(1)} collective-permute-done((f32[512,384]{0,1:T(8,128)S(1)}, f32[512,384]{0,1:T(8,128)S(1)}, u32[]{:S(2)}, u32[]{:S(2)}) %collective-permute-start.3) | collective-permute-done | bytes 786464 | tf_op jit(solution)/shard_map/ppermute | solution.py:12
  510.4 12.3 all-to-all-done.2
  545.0 11.7 cholesky.703
  563.5 19.9 %custom-call.51 = f32[2,128,128]{1,2,0:T(8,128)S(1)} custom-call(f32[2,128,128]{2,1,0:T(8,128)S(1)} %get-tuple-element.90), custom_call_target="InvertDiagBlocksLowerTriangular" | custom-call | tf_op jit(solution)/shard_map/jit(_solve_triangular)/triangular_solve | solution.py:16
  630.1 39.7 %custom-call.53 = f32[4,128,128]{1,2,0:T(8,128)S(1)} custom-call(f32[4,128,128]{2,1,0:T(8,128)S(1)} %get-tuple-element.91), custom_call_target="InvertDiagBlocksLowerTriangular" | custom-call | tf_op jit(solution)/shard_map/jit(_solve_triangular)/triangular_solve | solution.py:16
  674.9 35.1 %all-gather.12.cloned.1.call-done = f32[2,512,512]{2,1,0:T(8,128)} async-done(((f32[2,512,128]{2,1,0:T(8,128)}), f32[2,512,512]{2,1,0:T(8,128)}) %all-gather.12.cloned.1.call-update) | async-done | bytes 2097168 | tf_op jit(solution)/shard_map/all_gather | solution.py:69
  720.7 14.1 %collective-permute-done.5 = f32[512,384]{0,1:T(8,128)S(1)} collective-permute-done((f32[512,384]{0,1:T(8,128)S(1)}, f32[512,384]{0,1:T(8,128)S(1)}, u32[]{:S(2)}, u32[]{:S(2)}) %collective-permute-start.5) | collective-permute-done | bytes 786464 | tf_op jit(solution)/shard_map/ppermute | solution.py:12
  734.8 18.8 %collective-permute-done.6 = f32[512,384]{0,1:T(8,128)S(1)} collective-permute-done((f32[512,384]{0,1:T(8,128)S(1)}, f32[512,384]{0,1:T(8,128)S(1)}, u32[]{:S(2)}, u32[]{:S(2)}) %collective-permute-start.6) | collective-permute-done | bytes 786464 | tf_op jit(solution)/shard_map/ppermute | solution.py:12
  759.2 12.6 all-to-all-done.3
  794.1 11.7 cholesky.771
  812.6 19.9 %custom-call.55 = f32[2,128,128]{1,2,0:T(8,128)S(1)} custom-call(f32[2,128,128]{2,1,0:T(8,128)S(1)} %get-tuple-element.92), custom_call_target="InvertDiagBlocksLowerTriangular" | custom-call | tf_op jit(solution)/shard_map/jit(_solve_triangular)/triangular_solve | solution.py:16
  879.2 39.7 %custom-call.57 = f32[4,128,128]{1,2,0:T(8,128)S(1)} custom-call(f32[4,128,128]{2,1,0:T(8,128)S(1)} %get-tuple-element.93), custom_call_target="InvertDiagBlocksLowerTriangular" | custom-call | tf_op jit(solution)/shard_map/jit(_solve_triangular)/triangular_solve | solution.py:16
  924.0 33.2 %all-gather.14.cloned.1.call-done = f32[2,512,512]{2,1,0:T(8,128)} async-done(((f32[2,512,128]{2,1,0:T(8,128)}), f32[2,512,512]{2,1,0:T(8,128)}) %all-gather.14.cloned.1.call-update) | async-done | bytes 2097168 | tf_op jit(solution)/shard_map/all_gather | solution.py:69
  966.5 14.1 %collective-permute-done.7 = f32[512,384]{0,1:T(8,128)S(1)} collective-permute-done((f32[512,384]{0,1:T(8,128)S(1)}, f32[512,384]{0,1:T(8,128)S(1)}, u32[]{:S(2)}, u32[]{:S(2)}) %collective-permute-start.7) | collective-permute-done | bytes 786464 | tf_op jit(solution)/shard_map/ppermute | solution.py:12
  990.3 12.4 all-to-all-done.4
  1043.5 19.9 %custom-call.59 = f32[2,128,128]{1,2,0:T(8,128)S(1)} custom-call(f32[2,128,128]{2,1,0:T(8,128)S(1)} %get-tuple-element.94), custom_call_target="InvertDiagBlocksLowerTriangular" | custom-call | tf_op jit(solution)/shard_map/jit(_solve_triangular)/triangular_solve | solution.py:16
  1110.1 39.7 %custom-call.61 = f32[4,128,128]{1,2,0:T(8,128)S(1)} custom-call(f32[4,128,128]{2,1,0:T(8,128)S(1)} %get-tuple-element.95), custom_call_target="InvertDiagBlocksLowerTriangular" | custom-call | tf_op jit(solution)/shard_map/jit(_solve_triangular)/triangular_solve | solution.py:16
  1154.8 33.2 %all-gather.16.cloned.1.call-done = f32[2,512,512]{2,1,0:T(8,128)} async-done(((f32[2,512,128]{2,1,0:T(8,128)}), f32[2,512,512]{2,1,0:T(8,128)}) %all-gather.16.cloned.1.call-update) | async-done | bytes 2097168 | tf_op jit(solution)/shard_map/all_gather | solution.py:69
  1200.0 13.9 collective-permute-done.10
  1220.5 12.6 all-to-all-done.5
  1274.0 19.9 %custom-call.63 = f32[2,128,128]{1,2,0:T(8,128)S(1)} custom-call(f32[2,128,128]{2,1,0:T(8,128)S(1)} %get-tuple-element.96), custom_call_target="InvertDiagBlocksLowerTriangular" | custom-call | tf_op jit(solution)/shard_map/jit(_solve_triangular)/triangular_solve | solution.py:16
  1341.0 39.6 %custom-call.21 = f32[4,128,128]{1,2,0:T(8,128)S(1)} custom-call(f32[4,128,128]{2,1,0:T(8,128)S(1)} %get-tuple-element.31), custom_call_target="InvertDiagBlocksLowerTriangular" | custom-call | tf_op jit(solution)/shard_map/jit(_solve_triangular)/triangular_solve | solution.py:82
  (512 shorter events, 677.2 us)
Async XLA Ops:
  6.5 29.1 %all-gather.18.cloned.1.call-start = ((), (), s32[]{:S(2)}) async-start(), calls=%async_computation.11 | async-start | bytes 1310720 | tf_op jit(solution)/shard_map/all_gather | solution.py:47
  38.0 3.4 collective-permute-start
  41.5 5.5 copy-start.10
  43.4 16.8 %all-to-all-start = ((f32[4,512,128]{1,2,0:T(8,128)}), f32[4,512,128]{1,2,0:T(8,128)S(1)}, u32[]{:S(2)}, u32[]{:S(2)}) async-start(f32[4,512,128]{1,2,0:T(8,128)} %stack.42), calls=%async_computation | async-start | bytes 2097152 | tf_op jit(solution)/shard_map/all_to_all | solution.py:34
  46.9 203.6 %all-gather.8.cloned.1.call-start = ((), (), s32[]{:S(2)}) async-start(), calls=%async_computation.6 | async-start | bytes 2621440 | tf_op jit(solution)/shard_map/all_gather | solution.py:69
  47.1 35.1 %copy-start.6 = (f32[1,512,128]{1,2,0:T(8,128)}, f32[1,512,128]{1,2,0:T(8,128)S(1)}, u32[]{:S(2)}) copy-start(f32[1,512,128]{1,2,0:T(8,128)S(1)} %copy.10) | copy-start | bytes 786436
  254.8 7.3 copy-start.7
  255.0 3.2 collective-permute-start.1
  256.3 5.9 collective-permute-start.2
  263.6 14.8 %all-to-all-start.1 = ((f32[4,512,128]{1,2,0:T(8,128)}), f32[4,512,128]{1,2,0:T(8,128)S(1)}, u32[]{:S(2)}, u32[]{:S(2)}) async-start(f32[4,512,128]{1,2,0:T(8,128)} %stack.91), calls=%async_computation.1 | async-start | bytes 2097152 | tf_op jit(solution)/shard_map/all_to_all | solution.py:34
  267.5 209.9 %all-gather.10.cloned.1.call-start = ((), (), s32[]{:S(2)}) async-start(), calls=%async_computation.7 | async-start | bytes 2621440 | tf_op jit(solution)/shard_map/all_gather | solution.py:69
  481.7 23.1 %copy-start.1 = (f32[512,128]{0,1:T(8,128)S(1)}, f32[512,128]{0,1:T(8,128)}, u32[]{:S(2)}) copy-start(f32[512,128]{0,1:T(8,128)} %copy-done) | copy-start | bytes 786436
  481.8 18.8 %collective-permute-start.3 = (f32[512,384]{0,1:T(8,128)S(1)}, f32[512,384]{0,1:T(8,128)S(1)}, u32[]{:S(2)}, u32[]{:S(2)}) collective-permute-start(f32[512,384]{0,1:T(8,128)S(1)} %get-tuple-element.243), channel_id=1, source_target_pairs={{0,8},{4,12},{8,16},{12,20},{16,24},{20,28},{24,32},{28,36},{32,40... | collective-permute-start | bytes 2359304 | tf_op jit(solution)/shard_map/ppermute | solution.py:12
  485.3 19.5 %collective-permute-start.4 = (f32[512,384]{0,1:T(8,128)S(1)}, f32[512,384]{0,1:T(8,128)S(1)}, u32[]{:S(2)}, u32[]{:S(2)}) collective-permute-start(f32[512,384]{0,1:T(8,128)S(1)} %get-tuple-element.244), channel_id=1, source_target_pairs={{8,0},{12,4},{16,8},{20,12},{24,16},{28,20},{32,24},{36,28},{40,32... | collective-permute-start | bytes 2359304 | tf_op jit(solution)/shard_map/ppermute | solution.py:12
  505.1 5.3 copy-start.2
  506.2 16.5 %all-to-all-start.2 = ((f32[4,512,128]{1,2,0:T(8,128)}), f32[4,512,128]{1,2,0:T(8,128)S(1)}, u32[]{:S(2)}, u32[]{:S(2)}) async-start(f32[4,512,128]{1,2,0:T(8,128)} %stack.95), calls=%async_computation.2 | async-start | bytes 2097152 | tf_op jit(solution)/shard_map/all_to_all | solution.py:34
  510.1 199.8 %all-gather.12.cloned.1.call-start = ((), (), s32[]{:S(2)}) async-start(), calls=%async_computation.8 | async-start | bytes 2621440 | tf_op jit(solution)/shard_map/all_gather | solution.py:69
  714.3 39.3 %copy-start.3 = (f32[512,128]{0,1:T(8,128)S(1)}, f32[512,128]{0,1:T(8,128)}, u32[]{:S(2)}) copy-start(f32[512,128]{0,1:T(8,128)} %copy-done.2) | copy-start | bytes 786436
  714.5 20.3 %collective-permute-start.5 = (f32[512,384]{0,1:T(8,128)S(1)}, f32[512,384]{0,1:T(8,128)S(1)}, u32[]{:S(2)}, u32[]{:S(2)}) collective-permute-start(f32[512,384]{0,1:T(8,128)S(1)} %get-tuple-element.239), channel_id=1, source_target_pairs={{0,16},{4,20},{8,24},{12,28},{16,32},{20,36},{24,40},{28,44},{32,4... | collective-permute-start | bytes 2359304 | tf_op jit(solution)/shard_map/ppermute | solution.py:12
  719.4 34.2 %collective-permute-start.6 = (f32[512,384]{0,1:T(8,128)S(1)}, f32[512,384]{0,1:T(8,128)S(1)}, u32[]{:S(2)}, u32[]{:S(2)}) collective-permute-start(f32[512,384]{0,1:T(8,128)S(1)} %get-tuple-element.240), channel_id=1, source_target_pairs={{16,0},{20,4},{24,8},{28,12},{32,16},{36,20},{40,24},{44,28},{48,3... | collective-permute-start | bytes 2359304 | tf_op jit(solution)/shard_map/ppermute | solution.py:12
  755.0 16.8 %all-to-all-start.3 = ((f32[4,512,128]{1,2,0:T(8,128)}), f32[4,512,128]{1,2,0:T(8,128)S(1)}, u32[]{:S(2)}, u32[]{:S(2)}) async-start(f32[4,512,128]{1,2,0:T(8,128)} %stack.99), calls=%async_computation.3 | async-start | bytes 2097152 | tf_op jit(solution)/shard_map/all_to_all | solution.py:34
  758.9 198.3 %all-gather.14.cloned.1.call-start = ((), (), s32[]{:S(2)}) async-start(), calls=%async_computation.9 | async-start | bytes 2621440 | tf_op jit(solution)/shard_map/all_gather | solution.py:69
  961.6 23.2 %copy-start.5 = (f32[512,128]{0,1:T(8,128)S(1)}, f32[512,128]{0,1:T(8,128)}, u32[]{:S(2)}) copy-start(f32[512,128]{0,1:T(8,128)} %copy-done.4) | copy-start | bytes 786436
  961.7 18.9 %collective-permute-start.7 = (f32[512,384]{0,1:T(8,128)S(1)}, f32[512,384]{0,1:T(8,128)S(1)}, u32[]{:S(2)}, u32[]{:S(2)}) collective-permute-start(f32[512,384]{0,1:T(8,128)S(1)} %get-tuple-element.235), channel_id=1, source_target_pairs={{0,32},{4,36},{8,40},{12,44},{16,48},{20,52},{24,56},{28,60},{32,6... | collective-permute-start | bytes 2359304 | tf_op jit(solution)/shard_map/ppermute | solution.py:12
  965.2 19.5 %collective-permute-start.8 = (f32[512,384]{0,1:T(8,128)S(1)}, f32[512,384]{0,1:T(8,128)S(1)}, u32[]{:S(2)}, u32[]{:S(2)}) collective-permute-start(f32[512,384]{0,1:T(8,128)S(1)} %get-tuple-element.236), channel_id=1, source_target_pairs={{32,0},{36,4},{40,8},{44,12},{48,16},{52,20},{56,24},{60,28},{64,3... | collective-permute-start | bytes 2359304 | tf_op jit(solution)/shard_map/ppermute | solution.py:12
  985.0 5.3 copy-start.8
  986.1 16.5 %all-to-all-start.4 = ((f32[4,512,128]{1,2,0:T(8,128)}), f32[4,512,128]{1,2,0:T(8,128)S(1)}, u32[]{:S(2)}, u32[]{:S(2)}) async-start(f32[4,512,128]{1,2,0:T(8,128)} %stack.103), calls=%async_computation.4 | async-start | bytes 2097152 | tf_op jit(solution)/shard_map/all_to_all | solution.py:34
  990.1 198.0 %all-gather.16.cloned.1.call-start = ((), (), s32[]{:S(2)}) async-start(), calls=%async_computation.10 | async-start | bytes 2621440 | tf_op jit(solution)/shard_map/all_gather | solution.py:69
  1192.4 22.7 %copy-start.9 = (f32[512,128]{0,1:T(8,128)S(1)}, f32[512,128]{0,1:T(8,128)}, u32[]{:S(2)}) copy-start(f32[512,128]{0,1:T(8,128)} %copy-done.8) | copy-start | bytes 786436
  1192.5 21.3 %collective-permute-start.10 = (f32[512,384]{0,1:T(8,128)S(1)}, f32[512,384]{0,1:T(8,128)S(1)}, u32[]{:S(2)}, u32[]{:S(2)}) collective-permute-start(f32[512,384]{0,1:T(8,128)S(1)} %get-tuple-element.232), channel_id=1, source_target_pairs={{64,0},{68,4},{72,8},{76,12},{80,16},{84,20},{88,24},{92,28},{96,3... | collective-permute-start | bytes 2359304 | tf_op jit(solution)/shard_map/ppermute | solution.py:12
  1193.8 21.2 %collective-permute-start.9 = (f32[512,384]{0,1:T(8,128)S(1)}, f32[512,384]{0,1:T(8,128)S(1)}, u32[]{:S(2)}, u32[]{:S(2)}) collective-permute-start(f32[512,384]{0,1:T(8,128)S(1)} %get-tuple-element.231), channel_id=1, source_target_pairs={{0,64},{4,68},{8,72},{12,76},{16,80},{20,84},{24,88},{28,92},{32,9... | collective-permute-start | bytes 2359304 | tf_op jit(solution)/shard_map/ppermute | solution.py:12
  1216.4 16.7 %all-to-all-start.5 = ((f32[4,512,128]{1,2,0:T(8,128)}), f32[4,512,128]{1,2,0:T(8,128)S(1)}, u32[]{:S(2)}, u32[]{:S(2)}) async-start(f32[4,512,128]{1,2,0:T(8,128)} %stack.107), calls=%async_computation.5 | async-start | bytes 2097152 | tf_op jit(solution)/shard_map/all_to_all | solution.py:34
  (2 other events, 10.6 us)
Sparse Core Ops, SparseCore 0:
  9.0 26.5 all-gather.17
  212.1 38.3 all-gather.7
  430.7 46.6 all-gather.9
  675.0 34.9 all-gather.11
  924.1 33.0 all-gather.13
  1155.0 33.0 all-gather.15
